TPU v7x, 256 devices: a whole 4x4x8 slice. The times are simulated.
256 devices in a mesh: col: 32 (over x, y, core), row: 8 (over z).
Axes of the slice: x: 4, y: 4, z: 8, core: 2. Of those that a mesh axis runs over, the one named last changes fastest.
Arguments:
- weights: float32 [4096, 53248], P('row', 'col'), may hold values from -6 to 6
- factor: float32 [6, 512, 53248], P(None, 'row', 'col'), as said below
- diag_inverse: float32 [6, 4, 128, 128], replicated
- prune_mask: int32 [6, 32, 4], P(None, 'row'), may hold values 0 or 1
- panel_start: int32 [6], replicated, may hold values from 0 to 52736, as said below
Outputs:
- pruned: float32 [4096, 53248], P('row', 'col')
Inputs may be any that keep to these rules, and one draw needn't show every extreme that they name: `panel_start`: strictly increasing; each a multiple of 128; each panel lies within one block of 1664 columns, and no two panels in the same block. `factor`: row j of panel k is zero left of column panel_start[k] + j and positive on it.
All inputs are finite; a program needn't handle non-finite values. No bound on the sum of `prune_mask` on one device may be relied on, other than what follows from the above.
Results may differ from a plain program's by a relative error of at most 0.0001.
Values sent between devices are 32-bit elements; how exact they have to be, the bound alone decides.
No kernel may reach another device: no remote copies, remote signals or barrier semaphores. Data moves between devices by JAX's collectives and lax.ppermute only.
A program may use at most 192 MiB of HBM per device.

v0:
```python
import jax
import jax.numpy as jnp
from jax import lax
from jax.sharding import Mesh
from jax.sharding import PartitionSpec as P

TILE = 128
PANEL_TILES = 4
PW = 512
P_SIZE = 6
COL = ("col_0", "col_1", "col_2")


def cut_along(value, dim, devices):
    dims = value.shape
    tiles = value.reshape(*dims[:dim], devices, dims[dim] // devices, *dims[dim + 1 :])
    return jnp.moveaxis(tiles, dim, 0)


def sent_and_summed(value, axis, dim):
    tiles = cut_along(value, dim, lax.axis_size(axis))
    arrived = lax.all_to_all(tiles, axis, split_axis=0, concat_axis=0, tiled=True)
    return arrived.sum(axis=0)


def summed_rows(value, axes, dim):
    far, near = axes
    own = sent_and_summed(cut_along(value, dim, lax.axis_size(far)), near, dim + 1)
    return jnp.sum(lax.all_to_all(own, far, 0, 0, tiled=True), axis=0)


def filled_up(lines, devices):
    spare = -lines.shape[0] % devices
    if not spare:
        return lines
    return jnp.concatenate([lines, jnp.zeros((spare, *lines.shape[1:]), lines.dtype)])


def sent_to_all(value, axis):
    devices = lax.axis_size(axis)
    return lax.all_to_all(
        jnp.broadcast_to(value[None], (devices, *value.shape)), axis, 0, 0, tiled=True
    )


def laid_out(tiles, dim):
    dims = list(tiles.shape[1:])
    dims[dim] *= tiles.shape[0]
    return jnp.moveaxis(tiles, 0, dim).reshape(dims)


def gathered_by_axis(value, axes, dim):
    far, near = axes
    leading = sent_to_all(value, far)
    tiles = jnp.swapaxes(sent_to_all(leading, near), 0, 1)
    return laid_out(tiles.reshape(-1, *value.shape), dim)


def nested_sum(value, axes):
    lines = value.reshape(-1, value.shape[-1])
    own = summed_rows(filled_up(lines, lax.axis_size(axes[0]) * lax.axis_size(axes[1])), axes, 0)
    whole = gathered_by_axis(own, axes, 0)
    return whole[: len(lines)].reshape(value.shape)


def panel_errors(wpanel, ublock, dinv, rowmask):
    tiles = []
    for a in range(PANEL_TILES):
        acc = wpanel[:, a * TILE : (a + 1) * TILE]
        for b in range(a):
            acc = acc - jnp.dot(
                tiles[b],
                ublock[b * TILE : (b + 1) * TILE, a * TILE : (a + 1) * TILE],
                precision=lax.Precision.HIGHEST,
            )
        tiles.append(rowmask[:, a : a + 1] * jnp.dot(acc, dinv[a], precision=lax.Precision.HIGHEST))
    return jnp.concatenate(tiles, 1)


def shards(weights, factor, diag_inverse, prune_mask, panel_start):
    width = weights.shape[1]
    myself = lax.axis_index(COL)
    starts = TILE * jnp.arange(PANEL_TILES, dtype=jnp.int32)
    all_rows = lax.all_gather(factor, "row", axis=1, tiled=True)
    for k in range(P_SIZE):
        first = panel_start[k]
        owner = first // width
        shift_col = jnp.clip(first - myself * width, 0, width - PW)
        wpanel = lax.dynamic_slice_in_dim(weights, shift_col, PW, 1)
        rows_k = all_rows[k]
        ublock = lax.dynamic_slice_in_dim(rows_k, shift_col, PW, 1)
        rowmask = jnp.repeat(prune_mask[k].astype(jnp.float32), TILE, axis=0)
        errors = panel_errors(wpanel, ublock, diag_inverse[k], rowmask)
        owned = jnp.where(myself == owner, errors, jnp.zeros_like(errors))
        errors = nested_sum(owned, (("col_0", "col_1"), "col_2"))
        weights = weights - jnp.dot(errors, rows_k, precision=lax.Precision.HIGHEST)
        offset = myself * width + jnp.arange(width, dtype=jnp.int32) - first
        indicator = (
            (offset[None, :] >= starts[:, None]) & (offset[None, :] < starts[:, None] + TILE)
        ).astype(jnp.float32)
        prune = jnp.dot(rowmask, indicator, precision=lax.Precision.HIGHEST)
        weights = weights * (1.0 - prune)
    return weights


def solution(mesh):
    torus = Mesh(
        mesh.devices.reshape(4, 4, 2, mesh.shape["row"]), ("col_0", "col_1", "col_2", "row")
    )
    return jax.shard_map(
        shards,
        mesh=torus,
        in_specs=(P("row", COL), P(None, "row", COL), P(), P(None, "row", None), P()),
        out_specs=P("row", COL),
        check_vma=False,
    )
```

profile of v0, /device:TPU:1, one launch (start us, length us, event | category | flops | bytes accessed | tf_op | source)
XLA Modules:
  0.0 636.6 jit_solution(11401464521342157056)
XLA Ops:
  14.8 205.2 %all-gather.2.cloned.1.call-done = f32[6,512,1664]{2,1,0:T(8,128)} async-done(((f32[6,64,1664]{2,1,0:T(8,128)}), f32[6,512,1664]{2,1,0:T(8,128)}) %all-gather.2.cloned.1.call-update) | async-done | bytes 20447248 | tf_op jit(solution)/shard_map/all_gather | solution.py:84
  219.9 12.4 %fusion.180 = (f32[1,512,1664]{2,1,0:T(8,128)}, f32[1,512,1664]{2,1,0:T(8,128)}, f32[1,512,1664]{2,1,0:T(8,128)}, f32[1,512,1664]{2,1,0:T(8,128)}, f32[1,512,1664]{2,1,0:T(8,128)S(1)}, /*index=5*/f32[1,512,1664]{2,1,0:T(8,128)S(1)}) fusion(f32[6,512,1664]{2,1,0:T(8,128)} %all-gather.2.cloned.1.call-done), kind=kLoop, calls=%fused_computation.273 | loop fusion | bytes 40894464 | tf_op jit(solution)/shard_map/slice | solution.py:90
  243.0 5.0 all_to_all.120
  248.9 6.5 %all-to-all-start.1 = ((f32[16,16,512]{2,1,0:T(8,128)}), f32[16,16,512]{2,1,0:T(8,128)S(1)}, u32[]{:S(2)}, u32[]{:S(2)}) async-start(f32[16,16,512]{2,1,0:T(8,128)} %reduce_sum.108), calls=%async_computation.1 | async-start | bytes 1048576 | tf_op jit(solution)/shard_map/all_to_all | solution.py:29
  258.4 7.5 %all-to-all-done.1 = f32[16,16,512]{2,1,0:T(8,128)S(1)} async-done(((f32[16,16,512]{2,1,0:T(8,128)}), f32[16,16,512]{2,1,0:T(8,128)S(1)}, u32[]{:S(2)}, u32[]{:S(2)}) %all-to-all-start.1) | async-done | bytes 524320 | tf_op jit(solution)/shard_map/all_to_all | solution.py:29
  266.7 3.7 all-to-all-start.2
  273.8 5.9 all-to-all-done.2
  279.8 8.2 %all_to_all.121 = f32[2,16,16,512]{3,2,1,0:T(8,128)S(1)} all-to-all(f32[2,16,16,512]{3,2,1,0:T(8,128)S(1)} %broadcast_in_dim.38), channel_id=1, replica_groups=mesh['col_0'=4,'col_1'=4,'col_2'=2,'row'=8] {'col_2'}, dimensions={0} | all-to-all | bytes 2097152 | tf_op jit(solution)/shard_map/all_to_all | solution.py:41
  288.1 9.1 %bitcast_multiply_fusion.5 = f32[512,1664]{1,0:T(8,128)S(1)} fusion(f32[1664,512]{0,1:T(8,128)S(1)} %copy-done.8, f32[512,1664]{1,0:T(8,128)} %param.5, f32[512,512]{1,0:T(8,128)S(1)} %bitcast.335, f32[6,512,1664]{2,1,0:T(8,128)} %all-gather.2.cloned.1.call-done), kind=kOutput, calls=%fused_computation.15 | convolution fusion | flops 5237047296 | bytes 14680064 | tf_op jit(solution)/shard_map/dot_general | solution.py:96
  309.5 5.4 all_to_all.122
  317.1 4.2 all-to-all-start.5
  321.5 10.0 %all-to-all-done.5 = f32[16,16,512]{2,1,0:T(8,128)} async-done(((f32[16,16,512]{2,1,0:T(8,128)}), f32[16,16,512]{2,1,0:T(8,128)}, u32[]{:S(2)}, u32[]{:S(2)}) %all-to-all-start.5) | async-done | bytes 524320 | tf_op jit(solution)/shard_map/all_to_all | solution.py:29
  333.5 4.4 all-to-all-start.6
  341.8 3.3 fusion.136
  345.2 3.5 dynamic-slice_bitcast_fusion.2
  350.0 6.4 %all_to_all.123 = f32[2,16,16,512]{3,2,1,0:T(8,128)S(1)} all-to-all(f32[2,16,16,512]{3,2,1,0:T(8,128)S(1)} %broadcast_in_dim.41), channel_id=1, replica_groups=mesh['col_0'=4,'col_1'=4,'col_2'=2,'row'=8] {'col_2'}, dimensions={0} | all-to-all | bytes 2097152 | tf_op jit(solution)/shard_map/all_to_all | solution.py:41
  356.5 8.1 %bitcast_multiply_fusion.4 = f32[512,1664]{1,0:T(8,128)S(1)} fusion(f32[1664,512]{0,1:T(8,128)S(1)} %copy-done.7, f32[512,1664]{1,0:T(8,128)S(1)} %bitcast_multiply_fusion.5, f32[512,512]{1,0:T(8,128)S(1)} %bitcast.331, f32[6,512,1664]{2,1,0:T(8,128)} %all-gather.2.cloned.1.call-done), kind=kOutput, calls=%fused_computation.12 | convolution fusion | flops 5237047296 | bytes 14680064 | tf_op jit(solution)/shard_map/dot_general | solution.py:96
  377.0 4.6 all_to_all.124
  382.5 7.5 %all-to-all-start.9 = ((f32[16,16,512]{2,1,0:T(8,128)}), f32[16,16,512]{2,1,0:T(8,128)S(1)}, u32[]{:S(2)}, u32[]{:S(2)}) async-start(f32[16,16,512]{2,1,0:T(8,128)} %reduce_sum.112), calls=%async_computation.9 | async-start | bytes 1048576 | tf_op jit(solution)/shard_map/all_to_all | solution.py:29
  392.8 7.6 %all-to-all-done.9 = f32[16,16,512]{2,1,0:T(8,128)S(1)} async-done(((f32[16,16,512]{2,1,0:T(8,128)}), f32[16,16,512]{2,1,0:T(8,128)S(1)}, u32[]{:S(2)}, u32[]{:S(2)}) %all-to-all-start.9) | async-done | bytes 524320 | tf_op jit(solution)/shard_map/all_to_all | solution.py:29
  401.3 3.7 all-to-all-start.10
  405.0 3.3 fusion.132
  408.4 5.9 all-to-all-done.10
  414.4 7.7 %all_to_all.125 = f32[2,16,16,512]{3,2,1,0:T(8,128)S(1)} all-to-all(f32[2,16,16,512]{3,2,1,0:T(8,128)S(1)} %broadcast_in_dim.44), channel_id=1, replica_groups=mesh['col_0'=4,'col_1'=4,'col_2'=2,'row'=8] {'col_2'}, dimensions={0} | all-to-all | bytes 2097152 | tf_op jit(solution)/shard_map/all_to_all | solution.py:41
  422.2 9.1 %bitcast_multiply_fusion.3 = f32[512,1664]{1,0:T(8,128)S(1)} fusion(f32[1664,512]{0,1:T(8,128)} %fusion.132, f32[512,1664]{1,0:T(8,128)S(1)} %copy-done.3, f32[512,512]{1,0:T(8,128)S(1)} %bitcast.332, f32[6,512,1664]{2,1,0:T(8,128)} %all-gather.2.cloned.1.call-done), kind=kOutput, calls=%fused_computation.9 | convolution fusion | flops 5237047296 | bytes 14680064 | tf_op jit(solution)/shard_map/dot_general | solution.py:96
  443.6 5.4 all_to_all.126
  451.1 4.2 all-to-all-start.13
  455.5 10.0 %all-to-all-done.13 = f32[16,16,512]{2,1,0:T(8,128)} async-done(((f32[16,16,512]{2,1,0:T(8,128)}), f32[16,16,512]{2,1,0:T(8,128)}, u32[]{:S(2)}, u32[]{:S(2)}) %all-to-all-start.13) | async-done | bytes 524320 | tf_op jit(solution)/shard_map/all_to_all | solution.py:29
  467.5 4.3 all-to-all-start.14
  475.2 3.3 fusion.128
  478.5 3.5 dynamic-slice_bitcast_fusion
  483.3 6.6 %all_to_all.127 = f32[2,16,16,512]{3,2,1,0:T(8,128)S(1)} all-to-all(f32[2,16,16,512]{3,2,1,0:T(8,128)S(1)} %broadcast_in_dim.47), channel_id=1, replica_groups=mesh['col_0'=4,'col_1'=4,'col_2'=2,'row'=8] {'col_2'}, dimensions={0} | all-to-all | bytes 2097152 | tf_op jit(solution)/shard_map/all_to_all | solution.py:41
  490.1 8.1 %bitcast_multiply_fusion.2 = f32[512,1664]{1,0:T(8,128)S(1)} fusion(f32[1664,512]{0,1:T(8,128)S(1)} %copy-done.6, f32[512,1664]{1,0:T(8,128)S(1)} %bitcast_multiply_fusion.3, f32[512,512]{1,0:T(8,128)S(1)} %bitcast.333, f32[6,512,1664]{2,1,0:T(8,128)} %all-gather.2.cloned.1.call-done), kind=kOutput, calls=%fused_computation.6 | convolution fusion | flops 5237047296 | bytes 14680064 | tf_op jit(solution)/shard_map/dot_general | solution.py:96
  510.5 4.6 all_to_all.128
  516.0 6.8 %all-to-all-start.17 = ((f32[16,16,512]{2,1,0:T(8,128)}), f32[16,16,512]{2,1,0:T(8,128)S(1)}, u32[]{:S(2)}, u32[]{:S(2)}) async-start(f32[16,16,512]{2,1,0:T(8,128)} %reduce_sum.116), calls=%async_computation.17 | async-start | bytes 1048576 | tf_op jit(solution)/shard_map/all_to_all | solution.py:29
  525.3 7.9 %all-to-all-done.17 = f32[16,16,512]{2,1,0:T(8,128)S(1)} async-done(((f32[16,16,512]{2,1,0:T(8,128)}), f32[16,16,512]{2,1,0:T(8,128)S(1)}, u32[]{:S(2)}, u32[]{:S(2)}) %all-to-all-start.17) | async-done | bytes 524320 | tf_op jit(solution)/shard_map/all_to_all | solution.py:29
  534.1 4.2 all-to-all-start.18
  538.3 3.3 fusion.124
  541.7 5.8 all-to-all-done.18
  548.7 7.7 %all_to_all.129 = f32[2,16,16,512]{3,2,1,0:T(8,128)S(1)} all-to-all(f32[2,16,16,512]{3,2,1,0:T(8,128)S(1)} %broadcast_in_dim.50), channel_id=1, replica_groups=mesh['col_0'=4,'col_1'=4,'col_2'=2,'row'=8] {'col_2'}, dimensions={0} | all-to-all | bytes 2097152 | tf_op jit(solution)/shard_map/all_to_all | solution.py:41
  556.5 9.1 %bitcast_multiply_fusion.1 = f32[512,1664]{1,0:T(8,128)S(1)} fusion(f32[1664,512]{0,1:T(8,128)} %fusion.124, f32[512,1664]{1,0:T(8,128)S(1)} %copy-done.1, f32[512,512]{1,0:T(8,128)S(1)} %bitcast.334, f32[6,512,1664]{2,1,0:T(8,128)} %all-gather.2.cloned.1.call-done), kind=kOutput, calls=%fused_computation.3 | convolution fusion | flops 5237047296 | bytes 14680064 | tf_op jit(solution)/shard_map/dot_general | solution.py:96
  578.0 4.6 all_to_all.130
  582.6 13.3 %all_to_all.131 = f32[16,16,512]{2,1,0:T(8,128)S(1)} all-to-all(f32[16,16,512]{2,1,0:T(8,128)S(1)} %reduce_sum.118), channel_id=1, replica_groups=mesh['col_0'=4,'col_1'=4,'col_2'=2,'row'=8] {'col_0','col_1'}, dimensions={0} | all-to-all | bytes 1048576 | tf_op jit(solution)/shard_map/all_to_all | solution.py:29
  596.9 4.2 all-to-all-start.22
  601.7 3.3 fusion.120
  605.0 5.3 all-to-all-done.22
  611.5 7.7 %all_to_all.132 = f32[2,16,16,512]{3,2,1,0:T(8,128)S(1)} all-to-all(f32[2,16,16,512]{3,2,1,0:T(8,128)S(1)} %broadcast_in_dim.53), channel_id=1, replica_groups=mesh['col_0'=4,'col_1'=4,'col_2'=2,'row'=8] {'col_2'}, dimensions={0} | all-to-all | bytes 2097152 | tf_op jit(solution)/shard_map/all_to_all | solution.py:41
  619.3 10.2 %bitcast_multiply_fusion = f32[512,1664]{1,0:T(8,128)} fusion(f32[1664,512]{0,1:T(8,128)} %fusion.120, f32[512,1664]{1,0:T(8,128)S(1)} %copy-done.5, f32[512,512]{1,0:T(8,128)S(1)} %bitcast.330, f32[6,512,1664]{2,1,0:T(8,128)} %all-gather.2.cloned.1.call-done), kind=kOutput, calls=%fused_computation | convolution fusion | flops 5237047296 | bytes 14680064 | tf_op jit(solution)/shard_map/dot_general | solution.py:96
  (153 shorter events, 105.2 us)
Async XLA Ops:
  6.5 213.4 %all-gather.2.cloned.1.call-start = ((), (), s32[]{:S(2)}) async-start(), calls=%async_computation.24 | async-start | bytes 23003136 | tf_op jit(solution)/shard_map/all_gather | solution.py:84
  248.9 16.9 %all-to-all-start.1 = ((f32[16,16,512]{2,1,0:T(8,128)}), f32[16,16,512]{2,1,0:T(8,128)S(1)}, u32[]{:S(2)}, u32[]{:S(2)}) async-start(f32[16,16,512]{2,1,0:T(8,128)} %reduce_sum.108), calls=%async_computation.1 | async-start | bytes 1048576 | tf_op jit(solution)/shard_map/all_to_all | solution.py:29
  266.7 13.0 %all-to-all-start.2 = ((f32[16,16,512]{2,1,0:T(8,128)}), f32[16,16,512]{2,1,0:T(8,128)S(1)}, u32[]{:S(2)}, u32[]{:S(2)}) async-start(f32[16,16,512]{2,1,0:T(8,128)} %broadcast_in_dim.37), calls=%async_computation.2 | async-start | bytes 1048576 | tf_op jit(solution)/shard_map/all_to_all | solution.py:41
  279.7 8.4 %copy-start.8 = (f32[1664,512]{0,1:T(8,128)S(1)}, f32[1664,512]{0,1:T(8,128)}, u32[]{:S(2)}) copy-start(f32[1664,512]{0,1:T(8,128)} %fusion.140) | copy-start | bytes 10223620
  317.1 14.5 %all-to-all-start.5 = ((f32[16,16,512]{2,1,0:T(8,128)}), f32[16,16,512]{2,1,0:T(8,128)}, u32[]{:S(2)}, u32[]{:S(2)}) async-start(f32[16,16,512]{2,1,0:T(8,128)} %reduce_sum.110), calls=%async_computation.5 | async-start | bytes 1048576 | tf_op jit(solution)/shard_map/all_to_all | solution.py:29
  333.5 15.2 %all-to-all-start.6 = ((f32[16,16,512]{2,1,0:T(8,128)}), f32[16,16,512]{2,1,0:T(8,128)}, u32[]{:S(2)}, u32[]{:S(2)}) async-start(f32[16,16,512]{2,1,0:T(8,128)} %broadcast_in_dim.40), calls=%async_computation.6 | async-start | bytes 1048576 | tf_op jit(solution)/shard_map/all_to_all | solution.py:41
  348.7 7.9 %copy-start.7 = (f32[1664,512]{0,1:T(8,128)S(1)}, f32[1664,512]{0,1:T(8,128)}, u32[]{:S(2)}) copy-start(f32[1664,512]{0,1:T(8,128)} %fusion.136) | copy-start | bytes 10223620
  364.6 11.1 %copy-start.2 = (f32[512,1664]{1,0:T(8,128)}, f32[512,1664]{1,0:T(8,128)S(1)}, u32[]{:S(2)}) copy-start(f32[512,1664]{1,0:T(8,128)S(1)} %bitcast_multiply_fusion.4) | copy-start | bytes 10223620
  382.5 17.9 %all-to-all-start.9 = ((f32[16,16,512]{2,1,0:T(8,128)}), f32[16,16,512]{2,1,0:T(8,128)S(1)}, u32[]{:S(2)}, u32[]{:S(2)}) async-start(f32[16,16,512]{2,1,0:T(8,128)} %reduce_sum.112), calls=%async_computation.9 | async-start | bytes 1048576 | tf_op jit(solution)/shard_map/all_to_all | solution.py:29
  401.3 13.0 %all-to-all-start.10 = ((f32[16,16,512]{2,1,0:T(8,128)}), f32[16,16,512]{2,1,0:T(8,128)S(1)}, u32[]{:S(2)}, u32[]{:S(2)}) async-start(f32[16,16,512]{2,1,0:T(8,128)} %broadcast_in_dim.43), calls=%async_computation.10 | async-start | bytes 1048576 | tf_op jit(solution)/shard_map/all_to_all | solution.py:41
  414.3 7.9 %copy-start.3 = (f32[512,1664]{1,0:T(8,128)S(1)}, f32[512,1664]{1,0:T(8,128)}, u32[]{:S(2)}) copy-start(f32[512,1664]{1,0:T(8,128)} %copy-done.2) | copy-start | bytes 10223620
  451.1 14.5 %all-to-all-start.13 = ((f32[16,16,512]{2,1,0:T(8,128)}), f32[16,16,512]{2,1,0:T(8,128)}, u32[]{:S(2)}, u32[]{:S(2)}) async-start(f32[16,16,512]{2,1,0:T(8,128)} %reduce_sum.114), calls=%async_computation.13 | async-start | bytes 1048576 | tf_op jit(solution)/shard_map/all_to_all | solution.py:29
  467.5 14.5 %all-to-all-start.14 = ((f32[16,16,512]{2,1,0:T(8,128)}), f32[16,16,512]{2,1,0:T(8,128)}, u32[]{:S(2)}, u32[]{:S(2)}) async-start(f32[16,16,512]{2,1,0:T(8,128)} %broadcast_in_dim.46), calls=%async_computation.14 | async-start | bytes 1048576 | tf_op jit(solution)/shard_map/all_to_all | solution.py:41
  482.0 8.0 %copy-start.6 = (f32[1664,512]{0,1:T(8,128)S(1)}, f32[1664,512]{0,1:T(8,128)}, u32[]{:S(2)}) copy-start(f32[1664,512]{0,1:T(8,128)} %fusion.128) | copy-start | bytes 10223620
  498.2 11.1 %copy-start = (f32[512,1664]{1,0:T(8,128)}, f32[512,1664]{1,0:T(8,128)S(1)}, u32[]{:S(2)}) copy-start(f32[512,1664]{1,0:T(8,128)S(1)} %bitcast_multiply_fusion.2) | copy-start | bytes 10223620
  516.0 17.2 %all-to-all-start.17 = ((f32[16,16,512]{2,1,0:T(8,128)}), f32[16,16,512]{2,1,0:T(8,128)S(1)}, u32[]{:S(2)}, u32[]{:S(2)}) async-start(f32[16,16,512]{2,1,0:T(8,128)} %reduce_sum.116), calls=%async_computation.17 | async-start | bytes 1048576 | tf_op jit(solution)/shard_map/all_to_all | solution.py:29
  534.1 13.4 %all-to-all-start.18 = ((f32[16,16,512]{2,1,0:T(8,128)}), f32[16,16,512]{2,1,0:T(8,128)}, u32[]{:S(2)}, u32[]{:S(2)}) async-start(f32[16,16,512]{2,1,0:T(8,128)} %broadcast_in_dim.49), calls=%async_computation.18 | async-start | bytes 1048576 | tf_op jit(solution)/shard_map/all_to_all | solution.py:41
  541.7 14.8 %copy-start.1 = (f32[512,1664]{1,0:T(8,128)S(1)}, f32[512,1664]{1,0:T(8,128)}, u32[]{:S(2)}) copy-start(f32[512,1664]{1,0:T(8,128)} %copy-done) | copy-start | bytes 10223620
  565.6 11.1 %copy-start.4 = (f32[512,1664]{1,0:T(8,128)}, f32[512,1664]{1,0:T(8,128)S(1)}, u32[]{:S(2)}) copy-start(f32[512,1664]{1,0:T(8,128)S(1)} %bitcast_multiply_fusion.1) | copy-start | bytes 10223620
  596.9 13.4 %all-to-all-start.22 = ((f32[16,16,512]{2,1,0:T(8,128)}), f32[16,16,512]{2,1,0:T(8,128)}, u32[]{:S(2)}, u32[]{:S(2)}) async-start(f32[16,16,512]{2,1,0:T(8,128)} %broadcast_in_dim.52), calls=%async_computation.22 | async-start | bytes 1048576 | tf_op jit(solution)/shard_map/all_to_all | solution.py:41
  605.0 14.3 %copy-start.5 = (f32[512,1664]{1,0:T(8,128)S(1)}, f32[512,1664]{1,0:T(8,128)}, u32[]{:S(2)}) copy-start(f32[512,1664]{1,0:T(8,128)} %copy-done.4) | copy-start | bytes 10223620
Sparse Core Ops, SparseCore 0:
  9.1 210.7 all-gather.1
where the time goes:
time: 647 us; the launch traced here: 637 us
  waiting for transfers between devices  272 us (42%)
  matrix products  145 us (22%)
  blocking collectives  87.2 us (13%)
  starting transfers between devices  53.9 us (8%)
  local copies, waits for them, and re-layouts  34.7 us (5%)
  between operations  29.6 us (5%)
  other arithmetic  14.6 us (2%)
    all_gather x1, waiting for transfers between devices, shards(): all_rows = lax.all_gather(factor, 'row', axis=1, tiled=True)  205 us
    dot_general x6, matrix products, shards(): weights = weights - jnp.dot(errors, rows_k, precision=lax.Precision.HIGHEST)  53.7 us
    all_to_all x6, blocking collectives, sent_to_all(): lax.all_to_all(jnp.broadcast_to(value[None], (devices, *value.shape)), ax...  44.3 us
    all_to_all x5, waiting for transfers between devices, summed_rows(): return jnp.sum(lax.all_to_all(own, far, 0, 0, tiled=True), axis=0)  43 us
    dot_general x36, matrix products, panel_errors(): jnp.dot(tiles[b], ublock[b * TILE:(b + 1) * TILE, a * TILE:(a + 1) * TILE...  41.5 us
    dot_general x24, matrix products, panel_errors(): jnp.dot(acc, dinv[a], precision=lax.Precision.HIGHEST)  29.7 us
    all_to_all x6, blocking collectives, sent_and_summed(): lax.all_to_all(tiles, axis, split_axis=0, concat_axis=0, tiled=True)  29.6 us
    all_to_all x5, starting transfers between devices, summed_rows(): return jnp.sum(lax.all_to_all(own, far, 0, 0, tiled=True), axis=0)  29.3 us
  transfers between devices with their start and end apart: 12, of which 10 were waited for; matrix products, arithmetic and copies ran while one was open for 6% of the time, Pallas kernels for 0%

commit v1 on v0

--- a/solution.py
+++ b/solution.py
@@ -81,7 +81,9 @@
     width = weights.shape[1]
     myself = lax.axis_index(COL)
     starts = TILE * jnp.arange(PANEL_TILES, dtype=jnp.int32)
-    all_rows = lax.all_gather(factor, "row", axis=1, tiled=True)
+    all_rows = jnp.concatenate(
+        lax.all_to_all(jnp.stack([factor] * lax.axis_size("row")), "row", 0, 0), axis=1
+    )
     for k in range(P_SIZE):
         first = panel_start[k]
         owner = first // width

time: 647 us -> 886 us (1.37)
  waiting for transfers between devices: 272 us -> 529 us
  matrix products: 145 us -> 124 us
  between operations: 29.6 us -> 17.2 us
    all_to_all x0 -> x1, waiting for transfers between devices: none -> 441 us  [shards(): lax.all_to_all(jnp.stack([factor] * lax.axis_size('row')), 'row', 0, 0)]
    all_gather x1 -> x0, waiting for transfers between devices: 205 us -> none  [shards(): all_rows = lax.all_gather(factor, 'row', axis=1, tiled=True)]
    all_to_all x6, waiting for transfers between devices: 22.8 us -> 48 us  [sent_to_all(): lax.all_to_all(jnp.broadcast_to(value[None], (devices, *value.shape)), ax...]
    dot_general x6, matrix products: 53.7 us -> 38.1 us  [shards(): weights = weights - jnp.dot(errors, rows_k, precision=lax.Precision.HIGHEST)]
    another operation x0 -> x1, local copies, waits for them, and re-layouts: none -> 11 us  [shards(): jnp.stack([factor] * lax.axis_size('row'))]
    all_to_all x0 -> x1, starting transfers between devices: none -> 9.13 us  [shards(): lax.all_to_all(jnp.stack([factor] * lax.axis_size('row')), 'row', 0, 0)]
  transfers between devices with their start and end apart: 12 -> 12, of which waited for: 10 -> 12; matrix products, arithmetic and copies ran while one was open for 6% -> 1% of each run, Pallas kernels for 0% -> 0%
where the time goes in v1:
time: 886 us; the launch traced here: 876 us
  waiting for transfers between devices  529 us (60%)
  matrix products  124 us (14%)
  blocking collectives  89.2 us (10%)
  starting transfers between devices  59.5 us (7%)
  local copies, waits for them, and re-layouts  38.7 us (4%)
  other arithmetic  18.6 us (2%)
  between operations  17.2 us (2%)
    all_to_all x1, waiting for transfers between devices, shards(): lax.all_to_all(jnp.stack([factor] * lax.axis_size('row')), 'row', 0, 0)  441 us
    all_to_all x6, waiting for transfers between devices, sent_to_all(): lax.all_to_all(jnp.broadcast_to(value[None], (devices, *value.shape)), ax...  48 us
    all_to_all x6, blocking collectives, sent_to_all(): lax.all_to_all(jnp.broadcast_to(value[None], (devices, *value.shape)), ax...  45.1 us
    dot_general x36, matrix products, panel_errors(): jnp.dot(tiles[b], ublock[b * TILE:(b + 1) * TILE, a * TILE:(a + 1) * TILE...  40.5 us
    all_to_all x5, waiting for transfers between devices, summed_rows(): return jnp.sum(lax.all_to_all(own, far, 0, 0, tiled=True), axis=0)  40.4 us
    dot_general x6, matrix products, shards(): weights = weights - jnp.dot(errors, rows_k, precision=lax.Precision.HIGHEST)  38.1 us
    all_to_all x6, blocking collectives, sent_and_summed(): lax.all_to_all(tiles, axis, split_axis=0, concat_axis=0, tiled=True)  30.8 us
    dot_general x24, matrix products, panel_errors(): jnp.dot(acc, dinv[a], precision=lax.Precision.HIGHEST)  30.4 us
  transfers between devices with their start and end apart: 12, of which 12 were waited for; matrix products, arithmetic and copies ran while one was open for 1% of the time, Pallas kernels for 0%

profile of v1, /device:TPU:1, one launch (start us, length us, event | category | flops | bytes accessed | tf_op | source)
XLA Modules:
  0.0 875.9 jit_solution(6835439854173524779)
XLA Ops:
  0.0 11.0 %stack.2 = f32[8,6,64,1664]{3,2,1,0:T(8,128)} broadcast(f32[6,64,1664]{2,1,0:T(8,128)} %param.6), dimensions={1,2,3} | broadcast | bytes 23003136 | tf_op jit(solution)/shard_map/stack | solution.py:85
  11.0 9.1 %all-to-all-start = ((f32[8,6,64,1664]{3,2,1,0:T(8,128)}), f32[8,6,64,1664]{3,2,1,0:T(8,128)}, u32[]{:S(2)}, u32[]{:S(2)}) async-start(f32[8,6,64,1664]{3,2,1,0:T(8,128)} %stack.2), calls=%async_computation | async-start | bytes 40894464 | tf_op jit(solution)/shard_map/all_to_all | solution.py:85
  25.9 440.8 %all-to-all-done = f32[8,6,64,1664]{3,2,1,0:T(8,128)} async-done(((f32[8,6,64,1664]{3,2,1,0:T(8,128)}), f32[8,6,64,1664]{3,2,1,0:T(8,128)}, u32[]{:S(2)}, u32[]{:S(2)}) %all-to-all-start) | async-done | bytes 20447264 | tf_op jit(solution)/shard_map/all_to_all | solution.py:85
  466.7 12.6 %fusion.162 = (f32[1,8,64,1664]{3,2,0,1:T(8,128)}, f32[1,8,64,1664]{3,2,0,1:T(8,128)}, f32[1,8,64,1664]{3,2,0,1:T(8,128)}, f32[1,8,64,1664]{3,2,0,1:T(8,128)}, f...) fusion(f32[6,8,64,1664]{3,2,0,1:T(8,128)} %bitcast.6), kind=kLoop, calls=%fused_computation.261 | loop fusion | bytes 40894464 | tf_op jit(solution)/shard_map/slice | solution.py:92
  489.3 5.5 all_to_all.125
  497.0 6.8 all-to-all-start.2
  503.9 10.3 %all-to-all-done.2 = f32[16,16,512]{2,1,0:T(8,128)} async-done(((f32[16,16,512]{2,1,0:T(8,128)}), f32[16,16,512]{2,1,0:T(8,128)}, u32[]{:S(2)}, u32[]{:S(2)}) %all-to-all-start.2) | async-done | bytes 524320 | tf_op jit(solution)/shard_map/all_to_all | solution.py:29
  516.2 4.2 all-to-all-start.3
  524.0 5.6 all-to-all-done.3
  531.0 7.6 all_to_all.126
  538.7 6.4 fusion.170
  555.0 5.4 all_to_all.127
  562.6 4.2 all-to-all-start.6
  569.4 7.7 all-to-all-done.6
  579.0 4.7 all-to-all-start.7
  584.5 8.4 all-to-all-done.7
  594.1 7.5 all_to_all.128
  601.6 6.3 fusion.171
  623.1 5.4 all_to_all.129
  628.4 2.2 reduce_sum.112
  630.6 4.2 all-to-all-start.10
  637.8 7.3 all-to-all-done.10
  647.0 4.3 all-to-all-start.11
  652.0 8.5 all-to-all-done.11
  661.8 7.6 all_to_all.130
  669.5 6.4 fusion.172
  691.1 4.6 all_to_all.131
  696.6 3.6 all-to-all-start.14
  702.8 7.7 all-to-all-done.14
  711.4 4.9 all-to-all-start.15
  717.2 8.4 all-to-all-done.15
  726.7 7.5 all_to_all.132
  734.3 6.3 fusion.173
  755.8 5.4 all_to_all.133
  761.1 2.2 reduce_sum.116
  763.3 4.4 all-to-all-start.18
  770.6 7.3 all-to-all-done.18
  779.9 4.3 all-to-all-start.19
  784.9 8.5 all-to-all-done.19
  794.7 7.5 all_to_all.134
  802.2 6.3 fusion.174
  823.8 4.6 all_to_all.135
  828.5 13.4 %all_to_all.136 = f32[16,16,512]{2,1,0:T(8,128)S(1)} all-to-all(f32[16,16,512]{2,1,0:T(8,128)S(1)} %reduce_sum.118), channel_id=1, replica_groups=mesh['col_0'=4,'col_1'=4,'col_2'=2,'row'=8] {'col_0','col_1'}, dimensions={0} | all-to-all | bytes 1048576 | tf_op jit(solution)/shard_map/all_to_all | solution.py:29
  842.7 4.7 all-to-all-start.23
  848.1 8.5 all-to-all-done.23
  857.8 7.5 all_to_all.137
  865.4 6.3 fusion.175
  871.7 3.9 bitcast_multiply_fusion
  (164 shorter events, 110.9 us)
Async XLA Ops:
  11.0 9.1 %copy-start.15 = (s32[6]{0:T(128)S(1)}, s32[6]{0:T(128)}, u32[]{:S(2)}) copy-start(s32[6]{0:T(128)} %param.9) | copy-start | bytes 76
  11.0 12.4 %copy-start.14 = (s32[6,4,4]{0,2,1:T(4,128)S(1)}, s32[6,4,4]{0,2,1:T(4,128)}, u32[]{:S(2)}) copy-start(s32[6,4,4]{0,2,1:T(4,128)} %param.8) | copy-start | bytes 1156
  11.0 455.6 %all-to-all-start = ((f32[8,6,64,1664]{3,2,1,0:T(8,128)}), f32[8,6,64,1664]{3,2,1,0:T(8,128)}, u32[]{:S(2)}, u32[]{:S(2)}) async-start(f32[8,6,64,1664]{3,2,1,0:T(8,128)} %stack.2), calls=%async_computation | async-start | bytes 40894464 | tf_op jit(solution)/shard_map/all_to_all | solution.py:85
  466.7 12.6 %copy-start.12 = (f32[512,128]{1,0:T(8,128)S(1)}, f32[512,128]{1,0:T(8,128)}, u32[]{:S(2)}) copy-start(f32[512,128]{1,0:T(8,128)} %convolution_multiply_fusion.23) | copy-start | bytes 786436
  479.3 9.9 %copy-start.10 = (f32[1,8,64,1664]{3,2,0,1:T(8,128)}, f32[1,8,64,1664]{3,2,0,1:T(8,128)S(1)}, u32[]{:S(2)}) copy-start(f32[1,8,64,1664]{3,2,0,1:T(8,128)S(1)} %get-tuple-element.10) | copy-start | bytes 10223620
  497.0 17.3 %all-to-all-start.2 = ((f32[16,16,512]{2,1,0:T(8,128)}), f32[16,16,512]{2,1,0:T(8,128)}, u32[]{:S(2)}, u32[]{:S(2)}) async-start(f32[16,16,512]{2,1,0:T(8,128)} %reduce_sum.108), calls=%async_computation.2 | async-start | bytes 1048576 | tf_op jit(solution)/shard_map/all_to_all | solution.py:29
  516.2 13.4 %all-to-all-start.3 = ((f32[16,16,512]{2,1,0:T(8,128)}), f32[16,16,512]{2,1,0:T(8,128)}, u32[]{:S(2)}, u32[]{:S(2)}) async-start(f32[16,16,512]{2,1,0:T(8,128)} %broadcast_in_dim.37), calls=%async_computation.3 | async-start | bytes 1048576 | tf_op jit(solution)/shard_map/all_to_all | solution.py:41
  529.6 9.1 %copy-start.11 = (f32[1,8,64,1664]{3,2,0,1:T(8,128)S(1)}, f32[1,8,64,1664]{3,2,0,1:T(8,128)}, u32[]{:S(2)}) copy-start(f32[1,8,64,1664]{3,2,0,1:T(8,128)} %copy-done.10) | copy-start | bytes 10223620
  538.7 6.4 copy-start.13
  547.2 6.5 copy-start.2
  562.6 14.5 %all-to-all-start.6 = ((f32[16,16,512]{2,1,0:T(8,128)}), f32[16,16,512]{2,1,0:T(8,128)}, u32[]{:S(2)}, u32[]{:S(2)}) async-start(f32[16,16,512]{2,1,0:T(8,128)} %reduce_sum.110), calls=%async_computation.6 | async-start | bytes 1048576 | tf_op jit(solution)/shard_map/all_to_all | solution.py:29
  579.0 13.9 %all-to-all-start.7 = ((f32[16,16,512]{2,1,0:T(8,128)}), f32[16,16,512]{2,1,0:T(8,128)}, u32[]{:S(2)}, u32[]{:S(2)}) async-start(f32[16,16,512]{2,1,0:T(8,128)} %broadcast_in_dim.40), calls=%async_computation.7 | async-start | bytes 1048576 | tf_op jit(solution)/shard_map/all_to_all | solution.py:41
  601.6 6.4 copy-start.3
  630.6 14.5 %all-to-all-start.10 = ((f32[16,16,512]{2,1,0:T(8,128)}), f32[16,16,512]{2,1,0:T(8,128)}, u32[]{:S(2)}, u32[]{:S(2)}) async-start(f32[16,16,512]{2,1,0:T(8,128)} %reduce_sum.112), calls=%async_computation.10 | async-start | bytes 1048576 | tf_op jit(solution)/shard_map/all_to_all | solution.py:29
  647.0 13.5 %all-to-all-start.11 = ((f32[16,16,512]{2,1,0:T(8,128)}), f32[16,16,512]{2,1,0:T(8,128)}, u32[]{:S(2)}, u32[]{:S(2)}) async-start(f32[16,16,512]{2,1,0:T(8,128)} %broadcast_in_dim.43), calls=%async_computation.11 | async-start | bytes 1048576 | tf_op jit(solution)/shard_map/all_to_all | solution.py:41
  660.5 9.0 %copy-start.9 = (f32[1,8,64,1664]{3,2,0,1:T(8,128)S(1)}, f32[1,8,64,1664]{3,2,0,1:T(8,128)}, u32[]{:S(2)}) copy-start(f32[1,8,64,1664]{3,2,0,1:T(8,128)} %get-tuple-element.8) | copy-start | bytes 10223620
  678.0 11.7 %copy-start = (f32[512,1664]{1,0:T(8,128)}, f32[512,1664]{1,0:T(8,128)S(1)}, u32[]{:S(2)}) copy-start(f32[512,1664]{1,0:T(8,128)S(1)} %bitcast_multiply_fusion.3) | copy-start | bytes 10223620
  696.6 14.0 %all-to-all-start.14 = ((f32[16,16,512]{2,1,0:T(8,128)}), f32[16,16,512]{2,1,0:T(8,128)S(1)}, u32[]{:S(2)}, u32[]{:S(2)}) async-start(f32[16,16,512]{2,1,0:T(8,128)} %reduce_sum.114), calls=%async_computation.14 | async-start | bytes 1048576 | tf_op jit(solution)/shard_map/all_to_all | solution.py:29
  711.4 22.8 %copy-start.8 = (f32[1,8,64,1664]{3,2,0,1:T(8,128)S(1)}, f32[1,8,64,1664]{3,2,0,1:T(8,128)}, u32[]{:S(2)}) copy-start(f32[1,8,64,1664]{3,2,0,1:T(8,128)} %get-tuple-element.7) | copy-start | bytes 10223620
  711.4 14.1 %all-to-all-start.15 = ((f32[16,16,512]{2,1,0:T(8,128)}), f32[16,16,512]{2,1,0:T(8,128)}, u32[]{:S(2)}, u32[]{:S(2)}) async-start(f32[16,16,512]{2,1,0:T(8,128)} %broadcast_in_dim.46), calls=%async_computation.15 | async-start | bytes 1048576 | tf_op jit(solution)/shard_map/all_to_all | solution.py:41
  734.3 6.4 copy-start.1
  763.3 14.6 %all-to-all-start.18 = ((f32[16,16,512]{2,1,0:T(8,128)}), f32[16,16,512]{2,1,0:T(8,128)}, u32[]{:S(2)}, u32[]{:S(2)}) async-start(f32[16,16,512]{2,1,0:T(8,128)} %reduce_sum.116), calls=%async_computation.18 | async-start | bytes 1048576 | tf_op jit(solution)/shard_map/all_to_all | solution.py:29
  779.9 13.5 %all-to-all-start.19 = ((f32[16,16,512]{2,1,0:T(8,128)}), f32[16,16,512]{2,1,0:T(8,128)}, u32[]{:S(2)}, u32[]{:S(2)}) async-start(f32[16,16,512]{2,1,0:T(8,128)} %broadcast_in_dim.49), calls=%async_computation.19 | async-start | bytes 1048576 | tf_op jit(solution)/shard_map/all_to_all | solution.py:41
  793.4 8.9 %copy-start.7 = (f32[1,8,64,1664]{3,2,0,1:T(8,128)S(1)}, f32[1,8,64,1664]{3,2,0,1:T(8,128)}, u32[]{:S(2)}) copy-start(f32[1,8,64,1664]{3,2,0,1:T(8,128)} %get-tuple-element.6) | copy-start | bytes 10223620
  810.7 11.7 %copy-start.4 = (f32[512,1664]{1,0:T(8,128)}, f32[512,1664]{1,0:T(8,128)S(1)}, u32[]{:S(2)}) copy-start(f32[512,1664]{1,0:T(8,128)S(1)} %bitcast_multiply_fusion.1) | copy-start | bytes 10223620
  842.7 22.6 %copy-start.6 = (f32[1,8,64,1664]{3,2,0,1:T(8,128)S(1)}, f32[1,8,64,1664]{3,2,0,1:T(8,128)}, u32[]{:S(2)}) copy-start(f32[1,8,64,1664]{3,2,0,1:T(8,128)} %get-tuple-element.5) | copy-start | bytes 10223620
  842.7 13.9 %all-to-all-start.23 = ((f32[16,16,512]{2,1,0:T(8,128)}), f32[16,16,512]{2,1,0:T(8,128)}, u32[]{:S(2)}, u32[]{:S(2)}) async-start(f32[16,16,512]{2,1,0:T(8,128)} %broadcast_in_dim.52), calls=%async_computation.23 | async-start | bytes 1048576 | tf_op jit(solution)/shard_map/all_to_all | solution.py:41
  865.4 6.4 copy-start.5
